TPU v7x, 128 devices: a whole 4x4x4 slice. The times are simulated.
128 devices in a mesh: dev: 128 (over y, x, z, core).
Axes of the slice: x: 4, y: 4, z: 4, core: 2. Of those that a mesh axis runs over, the one named last changes fastest.
Arguments:
- params: float32 [59, 262144], P(None, 'dev'), as said below
- blocks: int32 [512, 32], P('dev'), may hold values from 0 to 2047, as said below
- counts: int32 [512], P('dev'), may hold values from 4 to 32, as said below
- pixel_grad: float32 [3, 524288], P(None, 'dev'), may hold values from -192 to 192
Outputs:
- param_grad: float32 [59, 262144], P(None, 'dev')
Inputs may be any that keep to these rules, and one draw needn't show every extreme that they name: Block b is owned by device b // 16. Within the tiles of one device no block appears twice, and for every owner exactly 1 of that device's 4 * 32 slots, used or not, name its blocks. `counts`: in every draw all tiles of some one device have 32 used slots. `params`: row 2, the depth, lies from 3 to 6; row 6 from 1 to 2; row 10 below -2.
All inputs are finite; a program needn't handle non-finite values.
Results may differ from a plain program's by a relative error of at most 0.0003.
Values sent between devices are 32-bit elements; how exact they have to be, the bound alone decides.
A program may use at most 128 MiB of HBM per device.

v0:
```python
import jax
import jax.numpy as jnp
from jax import lax
from jax.sharding import PartitionSpec as P

BLOCK = 128
TILE_SIDE = 32
TILES_X = 32
sh_zero = 0.28209479177387814
sh_one = 0.4886025119029199
sh_two = [
    1.0925484305920792,
    -1.0925484305920792,
    0.31539156525252005,
    -1.0925484305920792,
    0.5462742152960396,
]
sh_three = [
    -0.5900435899266435,
    2.890611442640554,
    -0.4570457994644658,
    0.3731763325901154,
    -0.4570457994644658,
    1.445305721320277,
    -0.5900435899266435,
]


def sh_basis(dir_x, dir_y, dir_z):
    sq_x = dir_x * dir_x
    sq_y = dir_y * dir_y
    sq_z = dir_z * dir_z
    return [
        sh_zero + 0.0 * dir_x,
        -sh_one * dir_y,
        sh_one * dir_z,
        -sh_one * dir_x,
        sh_two[0] * dir_x * dir_y,
        sh_two[1] * dir_y * dir_z,
        sh_two[2] * (2.0 * sq_z - sq_x - sq_y),
        sh_two[3] * dir_x * dir_z,
        sh_two[4] * (sq_x - sq_y),
        sh_three[0] * dir_y * (3.0 * sq_x - sq_y),
        sh_three[1] * dir_x * dir_y * dir_z,
        sh_three[2] * dir_y * (4.0 * sq_z - sq_x - sq_y),
        sh_three[3] * dir_z * (2.0 * sq_z - 3.0 * sq_x - 3.0 * sq_y),
        sh_three[4] * dir_x * (4.0 * sq_z - sq_x - sq_y),
        sh_three[5] * dir_z * (sq_x - sq_y),
        sh_three[6] * dir_x * (sq_x - 3.0 * sq_y),
    ]


def screen(params, focal_len, centre_x, centre_y):
    mean_x, mean_y, depths = (params[0], params[1], params[2])
    scales = jnp.exp(params[3:6])
    quat = params[6:10]
    quat = quat / jnp.sqrt(jnp.sum(quat * quat, axis=0))
    quat_r, quat_i, quat_j, quat_k = (quat[0], quat[1], quat[2], quat[3])
    rotation = [
        [
            1.0 - 2.0 * (quat_j * quat_j + quat_k * quat_k),
            2.0 * (quat_i * quat_j - quat_r * quat_k),
            2.0 * (quat_i * quat_k + quat_r * quat_j),
        ],
        [
            2.0 * (quat_i * quat_j + quat_r * quat_k),
            1.0 - 2.0 * (quat_i * quat_i + quat_k * quat_k),
            2.0 * (quat_j * quat_k - quat_r * quat_i),
        ],
        [
            2.0 * (quat_i * quat_k - quat_r * quat_j),
            2.0 * (quat_j * quat_k + quat_r * quat_i),
            1.0 - 2.0 * (quat_i * quat_i + quat_j * quat_j),
        ],
    ]
    inv_z = 1.0 / depths
    diag_jac = focal_len * inv_z
    side_x = -focal_len * mean_x * inv_z * inv_z
    side_y = -focal_len * mean_y * inv_z * inv_z
    upper = [
        (diag_jac * rotation[0][column] + side_x * rotation[2][column]) * scales[column]
        for column in range(3)
    ]
    lower = [
        (diag_jac * rotation[1][column] + side_y * rotation[2][column]) * scales[column]
        for column in range(3)
    ]
    cov_xx = upper[0] * upper[0] + upper[1] * upper[1] + upper[2] * upper[2] + 0.3
    cov_xy = upper[0] * lower[0] + upper[1] * lower[1] + upper[2] * lower[2]
    cov_yy = lower[0] * lower[0] + lower[1] * lower[1] + lower[2] * lower[2] + 0.3
    determ = cov_xx * cov_yy - cov_xy * cov_xy
    screen_u = focal_len * mean_x * inv_z + centre_x
    screen_v = focal_len * mean_y * inv_z + centre_y
    opacity = jax.nn.sigmoid(params[10])
    distance = jnp.sqrt(mean_x * mean_x + mean_y * mean_y + depths * depths)
    basis = sh_basis(mean_x / distance, mean_y / distance, depths / distance)
    colors = [
        0.5
        + sum((basis[harmonic] * params[11 + 16 * channel + harmonic] for harmonic in range(16)))
        for channel in range(3)
    ]
    features = jnp.stack(
        [screen_u, screen_v, cov_yy / determ, -cov_xy / determ, cov_xx / determ, opacity] + colors,
        axis=0,
    )
    return features.reshape(9, -1, BLOCK).transpose(1, 0, 2)


def coords_of(tile_id, positions):
    pix_x = (tile_id % TILES_X * TILE_SIDE + positions % TILE_SIDE).astype(jnp.float32) + 0.5
    pix_y = (tile_id // TILES_X * TILE_SIDE + positions // TILE_SIDE).astype(jnp.float32) + 0.5
    return (pix_x, pix_y)


def pixel_coords(tile_id):
    return coords_of(tile_id, jnp.arange(TILE_SIDE * TILE_SIDE, dtype=jnp.int32))


def pair_terms(feature, pix_x, pix_y):
    off_x = pix_x[:, None] - feature[0][None, :]
    off_y = pix_y[:, None] - feature[1][None, :]
    exponent = (
        -0.5 * (feature[2][None, :] * off_x * off_x + feature[4][None, :] * off_y * off_y)
        - feature[3][None, :] * off_x * off_y
    )
    falloff = jnp.exp(exponent)
    return (off_x, off_y, falloff, feature[5][None, :] * falloff)


def tile_gradients(listed, live_count, cotangent, pix_x, pix_y):
    precise = lax.Precision.HIGHEST
    pixels = pix_x.shape[0]

    def forward(slot_idx, state_in):
        log_trans, colors = state_in
        feature = listed[slot_idx]
        alphas = pair_terms(feature, pix_x, pix_y)[3]
        log_keep = jnp.log(1.0 - alphas)
        before = jnp.cumsum(log_keep, axis=1) - log_keep
        weight = jnp.exp(log_trans[:, None] + before) * alphas
        colors = colors + jnp.dot(weight, feature[6:9].T, precision=precise)
        return (log_trans + jnp.sum(log_keep, axis=1), colors)

    start_state = (jnp.zeros((pixels,), jnp.float32), jnp.zeros((pixels, 3), jnp.float32))
    image = lax.fori_loop(0, live_count, forward, start_state)[1]

    def backward(slot_idx, state_in):
        log_trans, done, gradients = state_in
        feature = listed[slot_idx]
        off_x, off_y, falloff, alphas = pair_terms(feature, pix_x, pix_y)
        log_keep = jnp.log(1.0 - alphas)
        before = jnp.cumsum(log_keep, axis=1) - log_keep
        transmit = jnp.exp(log_trans[:, None] + before)
        weight = transmit * alphas
        dalpha = jnp.zeros_like(alphas)
        for channel in range(3):
            shaded = weight * feature[6 + channel][None, :]
            behind = (image[:, channel] - done[:, channel])[:, None] - jnp.cumsum(shaded, axis=1)
            dalpha = dalpha + cotangent[channel][:, None] * (
                transmit * feature[6 + channel][None, :] - behind / (1.0 - alphas)
            )
        dcolor = jnp.dot(cotangent, weight, precision=precise)
        dpower = dalpha * alphas
        sums_list = [
            jnp.sum(dpower * (feature[2][None, :] * off_x + feature[3][None, :] * off_y), axis=0),
            jnp.sum(dpower * (feature[3][None, :] * off_x + feature[4][None, :] * off_y), axis=0),
            -0.5 * jnp.sum(dpower * off_x * off_x, axis=0),
            -jnp.sum(dpower * off_x * off_y, axis=0),
            -0.5 * jnp.sum(dpower * off_y * off_y, axis=0),
            jnp.sum(dalpha * falloff, axis=0),
        ]
        block_grad = jnp.concatenate([jnp.stack(sums_list, axis=0), dcolor], axis=0)
        gradients = lax.dynamic_update_index_in_dim(gradients, block_grad, slot_idx, 0)
        done = done + jnp.dot(weight, feature[6:9].T, precision=precise)
        return (log_trans + jnp.sum(log_keep, axis=1), done, gradients)

    return lax.fori_loop(
        0, live_count, backward, (start_state[0], start_state[1], jnp.zeros_like(listed))
    )[2]


def body(params, blocks, counts, pixel_grad):
    tiles_dev = counts.shape[0]
    devices = lax.axis_size("dev")
    image_width = TILES_X * TILE_SIDE
    height = devices * tiles_dev // TILES_X * TILE_SIDE
    local_feat, pullback = jax.vjp(
        lambda values: screen(values, float(image_width), image_width / 2.0, height / 2.0), params
    )
    flat_ids = blocks.reshape(-1)
    pixels = TILE_SIDE * TILE_SIDE
    cotangent = pixel_grad.reshape(3, tiles_dev, pixels).transpose(1, 0, 2)
    first_tile = lax.axis_index("dev") * tiles_dev
    all_feat = lax.all_gather(local_feat, "dev", axis=0, tiled=True)

    def one_tile(tile_args):
        tile_num, tile_feat, live_count, tile_cot = tile_args
        pix_x, pix_y = pixel_coords(first_tile + tile_num)
        return tile_gradients(tile_feat, live_count, tile_cot, pix_x, pix_y)

    gradients = lax.map(
        one_tile, (jnp.arange(tiles_dev, dtype=jnp.int32), all_feat[blocks], counts, cotangent)
    )
    dense_grad = jnp.zeros_like(all_feat).at[flat_ids].add(gradients.reshape(-1, 9, BLOCK))
    feature_grad = lax.psum_scatter(dense_grad, "dev", scatter_dimension=0, tiled=True)
    return pullback(feature_grad)[0]


def solution(mesh):
    return jax.shard_map(
        body,
        mesh=mesh,
        in_specs=(P(None, "dev"), P("dev", None), P("dev"), P(None, "dev")),
        out_specs=P(None, "dev"),
        check_vma=False,
    )
```

profile of v0, /device:TPU:0, one launch (start us, length us, event | category | flops | bytes accessed | tf_op | source)
XLA Modules:
  0.0 2045.2 jit_solution(7160727513263844686)
XLA Ops:
  8.3 1.9 add_add_fusion.15
  10.2 1.9 add_add_fusion.16
  12.1 1.8 add_add_fusion.17
  14.9 1.8 fusion.145
  20.1 76.5 %all-gather.2.cloned.1.call-done = f32[2048,9,128]{2,0,1:T(8,128)} async-done(((f32[16,9,128]{2,0,1:T(8,128)}), f32[2048,9,128]{2,0,1:T(8,128)}) %all-gather.2.cloned.1.call-update) | async-done | bytes 9437200 | tf_op jit(solution)/shard_map/all_gather | solution.py:194
  96.6 12.8 copy.7
  109.4 7.4 gather_fusion
  117.3 464.8 %while.67 = (s32[]{:T(128)}, f32[4,32,9,128]{3,2,1,0:T(8,128)}, s32[4]{0:T(128)}, f32[4,32,9,128]{3,2,1,0:T(8,128)}, s32[4]{0:T(128)}, /*index=5*/s32[]{:T(128)}...) while((s32[]{:T(128)}, f32[4,32,9,128]{3,2,1,0:T(8,128)}, ...), condition=%wide.region_19.20_spmd, body=%wide.region_1.19_spmd.sunk | while | flops 113947312 | bytes 16455790 | solution.py:201
  118.5 1.3 dynamic_slice.48
  122.3 24.7 %while.68 = (s32[]{:T(128)}, f32[1024]{0:T(1024)S(1)}, f32[1024,3]{0,1:T(4,128)S(1)}, s32[]{:T(128)}, f32[32,9,128]{2,1,0:T(8,128)S(1)}, /*index=5*/s32[]{:T(128...) while((s32[]{:T(128)}, f32[1024]{0:T(1024)S(1)}, ...), condition=%wide.region_5.5_spmd.clone, body=%wide.region_2.4_spmd.clone.sunk | while | flops 25318408 | bytes 2185531 | solution.py:145
  147.0 69.4 %while.69 = (s32[]{:T(128)}, f32[1024]{0:T(1024)S(1)}, f32[1024,3]{0,1:T(4,128)S(1)}, f32[32,9,128]{2,1,0:T(8,128)S(1)}, s32[]{:T(128)}, /*index=5*/f32[32,9,128...) while((s32[]{:T(128)}, f32[1024]{0:T(1024)S(1)}, ...), condition=%wide.region_18.18_spmd.clone, body=%wide.region_6.17_spmd.clone.sunk | while | flops 88628880 | bytes 13360023 | solution.py:177
  218.4 1.3 dynamic_slice.48
  222.2 29.5 %while.68 = (s32[]{:T(128)}, f32[1024]{0:T(1024)S(1)}, f32[1024,3]{0,1:T(4,128)S(1)}, s32[]{:T(128)}, f32[32,9,128]{2,1,0:T(8,128)S(1)}, /*index=5*/s32[]{:T(128...) while((s32[]{:T(128)}, f32[1024]{0:T(1024)S(1)}, ...), condition=%wide.region_5.5_spmd.clone, body=%wide.region_2.4_spmd.clone.sunk | while | flops 25318408 | bytes 2185531 | solution.py:145
  251.7 83.2 %while.69 = (s32[]{:T(128)}, f32[1024]{0:T(1024)S(1)}, f32[1024,3]{0,1:T(4,128)S(1)}, f32[32,9,128]{2,1,0:T(8,128)S(1)}, s32[]{:T(128)}, /*index=5*/f32[32,9,128...) while((s32[]{:T(128)}, f32[1024]{0:T(1024)S(1)}, ...), condition=%wide.region_18.18_spmd.clone, body=%wide.region_6.17_spmd.clone.sunk | while | flops 88628880 | bytes 13360023 | solution.py:177
  336.9 1.3 dynamic_slice.48
  340.7 24.7 %while.68 = (s32[]{:T(128)}, f32[1024]{0:T(1024)S(1)}, f32[1024,3]{0,1:T(4,128)S(1)}, s32[]{:T(128)}, f32[32,9,128]{2,1,0:T(8,128)S(1)}, /*index=5*/s32[]{:T(128...) while((s32[]{:T(128)}, f32[1024]{0:T(1024)S(1)}, ...), condition=%wide.region_5.5_spmd.clone, body=%wide.region_2.4_spmd.clone.sunk | while | flops 25318408 | bytes 2185531 | solution.py:145
  365.4 69.4 %while.69 = (s32[]{:T(128)}, f32[1024]{0:T(1024)S(1)}, f32[1024,3]{0,1:T(4,128)S(1)}, f32[32,9,128]{2,1,0:T(8,128)S(1)}, s32[]{:T(128)}, /*index=5*/f32[32,9,128...) while((s32[]{:T(128)}, f32[1024]{0:T(1024)S(1)}, ...), condition=%wide.region_18.18_spmd.clone, body=%wide.region_6.17_spmd.clone.sunk | while | flops 88628880 | bytes 13360023 | solution.py:177
  440.6 36.7 %while.68 = (s32[]{:T(128)}, f32[1024]{0:T(1024)S(1)}, f32[1024,3]{0,1:T(4,128)S(1)}, s32[]{:T(128)}, f32[32,9,128]{2,1,0:T(8,128)S(1)}, /*index=5*/s32[]{:T(128...) while((s32[]{:T(128)}, f32[1024]{0:T(1024)S(1)}, ...), condition=%wide.region_5.5_spmd.clone, body=%wide.region_2.4_spmd.clone.sunk | while | flops 25318408 | bytes 2185531 | solution.py:145
  477.4 103.9 %while.69 = (s32[]{:T(128)}, f32[1024]{0:T(1024)S(1)}, f32[1024,3]{0,1:T(4,128)S(1)}, f32[32,9,128]{2,1,0:T(8,128)S(1)}, s32[]{:T(128)}, /*index=5*/f32[32,9,128...) while((s32[]{:T(128)}, f32[1024]{0:T(1024)S(1)}, ...), condition=%wide.region_18.18_spmd.clone, body=%wide.region_6.17_spmd.clone.sunk | while | flops 88628880 | bytes 13360023 | solution.py:177
  582.1 6.0 broadcast_in_dim.29
  588.1 14.4 scatter_fusion
  602.6 1423.9 %reduce-scatter.2.cloned.1.call-done = f32[16,9,128]{2,1,0:T(8,128)} async-done(((f32[2048,9,128]{2,1,0:T(8,128)}), f32[16,9,128]{2,1,0:T(8,128)}) %reduce-scatter.2.cloned.1.call-update) | async-done | bytes 73744 | tf_op jit(solution)/shard_map/reduce_scatter | solution.py:205
  2031.3 1.9 fusion.80
  2036.4 2.0 pad_add_fusion
  (1373 shorter events, 406.8 us)
Async XLA Ops:
  6.5 90.1 %all-gather.2.cloned.1.call-start = ((), (), s32[]{:S(2)}) async-start(), calls=%async_computation.1 | async-start | bytes 9510912 | tf_op jit(solution)/shard_map/all_gather | solution.py:194
  17.8 0.6 copy-start.2
  18.4 2008.0 %reduce-scatter.2.cloned.1.call-start = ((), (), s32[]{:S(2)}) async-start(), calls=%async_computation.2 | async-start | bytes 16908288 | tf_op jit(solution)/shard_map/reduce_scatter | solution.py:205
  582.0 6.1 copy-start.1
  582.0 1446.6 %copy-start.10 = (f32[1,2048]{1,0:T(1,128)S(1)}, f32[1,2048]{1,0:T(1,128)}, u32[]{:S(2)}) copy-start(f32[1,2048]{1,0:T(1,128)} %get-tuple-element.361) | copy-start | bytes 24580
  582.0 1448.5 %copy-start.4 = (f32[1,2048]{1,0:T(1,128)S(1)}, f32[1,2048]{1,0:T(1,128)}, u32[]{:S(2)}) copy-start(f32[1,2048]{1,0:T(1,128)} %get-tuple-element.363) | copy-start | bytes 24580
  582.0 1448.6 %copy-start.5 = (f32[1,2048]{1,0:T(1,128)S(1)}, f32[1,2048]{1,0:T(1,128)}, u32[]{:S(2)}) copy-start(f32[1,2048]{1,0:T(1,128)} %get-tuple-element.365) | copy-start | bytes 24580
  582.0 1448.6 %copy-start.6 = (f32[1,2048]{1,0:T(1,128)S(1)}, f32[1,2048]{1,0:T(1,128)}, u32[]{:S(2)}) copy-start(f32[1,2048]{1,0:T(1,128)} %get-tuple-element.367) | copy-start | bytes 24580
  582.0 1448.6 %copy-start.7 = (f32[1,2048]{1,0:T(1,128)S(1)}, f32[1,2048]{1,0:T(1,128)}, u32[]{:S(2)}) copy-start(f32[1,2048]{1,0:T(1,128)} %get-tuple-element.371) | copy-start | bytes 24580
  582.1 1448.6 %copy-start.8 = (f32[1,2048]{1,0:T(1,128)S(1)}, f32[1,2048]{1,0:T(1,128)}, u32[]{:S(2)}) copy-start(f32[1,2048]{1,0:T(1,128)} %get-tuple-element.374) | copy-start | bytes 24580
  582.1 1448.6 %copy-start.9 = (f32[1,2048]{1,0:T(1,128)S(1)}, f32[1,2048]{1,0:T(1,128)}, u32[]{:S(2)}) copy-start(f32[1,2048]{1,0:T(1,128)} %get-tuple-element.377) | copy-start | bytes 24580
  582.1 1449.0 %copy-start = (f32[59,2048]{1,0:T(8,128)S(1)}, f32[59,2048]{1,0:T(8,128)}, u32[]{:S(2)}) copy-start(f32[59,2048]{1,0:T(8,128)} %param.10) | copy-start | bytes 1449988
  582.1 1449.1 %copy-start.3 = (f32[1,2048]{1,0:T(1,128)S(1)}, f32[1,2048]{1,0:T(1,128)}, u32[]{:S(2)}) copy-start(f32[1,2048]{1,0:T(1,128)} %get-tuple-element.364) | copy-start | bytes 24580
Sparse Core Ops, SparseCore 0:
  18.6 77.9 all-gather.1
  602.7 1423.7 reduce-scatter.1
where the time goes:
time: 2050 us
  waiting for transfers between devices  1500 us (73%)
  other arithmetic  321 us (16%)
  matrix products  83.6 us (4%)
  loops' own time  68.4 us (3%)
  local copies, waits for them, and re-layouts  58 us (3%)
    reduce_scatter x1, waiting for transfers between devices, body(): lax.psum_scatter(dense_grad, 'dev', scatter_dimension=0, tiled=True)  1420 us
    all_gather x1, waiting for transfers between devices, body(): all_feat = lax.all_gather(local_feat, 'dev', axis=0, tiled=True)  76.5 us
    another operation x141, other arithmetic, backward(): jnp.cumsum(shaded, axis=1)  68.6 us
    mul x47, other arithmetic, backward(): dpower = dalpha * alphas  48.8 us
    reduce_sum x47, other arithmetic, backward(): jnp.sum(dpower * (feature[3][None, :] * off_x + feature[4][None, :] * off...  44 us
  transfers between devices with their start and end apart: 2, of which 2 were waited for; matrix products, arithmetic and copies ran while one was open for 0% of the time, Pallas kernels for 0%

commit v1 on v0

--- a/solution.py
+++ b/solution.py
@@ -180,6 +180,11 @@
 
 
 def body(params, blocks, counts, pixel_grad):
+
+    def tails_list(tile_in, axis_id):
+        raw_out = jnp.stack(jax.lax.psum(1, axis_id) * [tile_in], axis=0)
+        return jnp.concatenate(jax.lax.all_to_all(raw_out, axis_id, 0, 0), axis=0)
+
     tiles_dev = counts.shape[0]
     devices = lax.axis_size("dev")
     image_width = TILES_X * TILE_SIDE
@@ -191,7 +196,7 @@
     pixels = TILE_SIDE * TILE_SIDE
     cotangent = pixel_grad.reshape(3, tiles_dev, pixels).transpose(1, 0, 2)
     first_tile = lax.axis_index("dev") * tiles_dev
-    all_feat = lax.all_gather(local_feat, "dev", axis=0, tiled=True)
+    all_feat = tails_list(local_feat, "dev")
 
     def one_tile(tile_args):
         tile_num, tile_feat, live_count, tile_cot = tile_args

time: 2050 us -> 2120 us (1.034)
  waiting for transfers between devices: 1500 us -> 1540 us
    all_to_all x0 -> x1, waiting for transfers between devices: none -> 115 us  [tails_list(): return jnp.concatenate(jax.lax.all_to_all(raw_out, axis_id, 0, 0), axis=0)]
    all_gather x1 -> x0, waiting for transfers between devices: 76.5 us -> none  [body(): all_feat = lax.all_gather(local_feat, 'dev', axis=0, tiled=True)]
    reshape x0 -> x1, local copies, waits for them, and re-layouts: none -> 22.5 us  [tails_list(): return jnp.concatenate(jax.lax.all_to_all(raw_out, axis_id, 0, 0), axis=0)]
where the time goes in v1:
time: 2120 us
  waiting for transfers between devices  1540 us (73%)
  other arithmetic  321 us (15%)
  matrix products  83.6 us (4%)
  loops' own time  72.5 us (3%)
  local copies, waits for them, and re-layouts  69.9 us (3%)
    reduce_scatter x1, waiting for transfers between devices, body(): lax.psum_scatter(dense_grad, 'dev', scatter_dimension=0, tiled=True)  1430 us
    all_to_all x1, waiting for transfers between devices, tails_list(): return jnp.concatenate(jax.lax.all_to_all(raw_out, axis_id, 0, 0), axis=0)  115 us
    another operation x141, other arithmetic, backward(): jnp.cumsum(shaded, axis=1)  68.6 us
    mul x47, other arithmetic, backward(): dpower = dalpha * alphas  48.8 us
    reduce_sum x47, other arithmetic, backward(): jnp.sum(dpower * (feature[3][None, :] * off_x + feature[4][None, :] * off...  44 us
  transfers between devices with their start and end apart: 2, of which 2 were waited for; matrix products, arithmetic and copies ran while one was open for 0% of the time, Pallas kernels for 0%

profile of v1, /device:TPU:0, one launch (start us, length us, event | category | flops | bytes accessed | tf_op | source)
XLA Modules:
  0.0 2116.9 jit_solution(13888098301883710079)
XLA Ops:
  8.4 2.5 add_add_fusion.15
  10.9 1.7 add_add_fusion.16
  12.6 1.8 add_add_fusion.17
  16.6 1.9 fusion.145
  19.6 4.2 stack.38
  23.9 11.6 all-to-all-start
  35.8 114.9 %all-to-all-done = f32[128,16,9,128]{3,1,2,0:T(8,128)} async-done(((f32[128,16,9,128]{3,1,2,0:T(8,128)}), f32[128,16,9,128]{3,1,2,0:T(8,128)}, u32[]{:S(2)}, u32[]{:S(2)}) %all-to-all-start) | async-done | bytes 9437216 | tf_op jit(solution)/shard_map/all_to_all | solution.py:186
  150.7 4.6 copy.10
  155.3 22.5 %copy.11 = f32[2048,9,128]{2,1,0:T(8,128)} copy(f32[2048,9,128]{2,0,1:T(8,128)S(1)} %bitcast.306) | data formatting | bytes 18874368 | tf_op jit(solution)/shard_map/reshape | solution.py:186
  177.8 7.4 gather_fusion
  185.2 463.2 %while.67 = (s32[]{:T(128)}, f32[4,32,9,128]{3,2,1,0:T(8,128)}, s32[4]{0:T(128)S(1)}, f32[4,32,9,128]{3,2,1,0:T(8,128)}, s32[4]{0:T(128)S(1)}, /*index=5*/s32[]{...) while((s32[]{:T(128)}, f32[4,32,9,128]{3,2,1,0:T(8,128)}, ...), condition=%wide.region_19.20_spmd, body=%wide.region_1.19_spmd.sunk | while | flops 113947312 | bytes 16455790 | solution.py:206
  188.7 25.2 %while.68 = (s32[]{:T(128)}, f32[1024]{0:T(1024)S(1)}, f32[1024,3]{0,1:T(4,128)S(1)}, s32[]{:T(128)}, f32[32,9,128]{2,1,0:T(8,128)S(1)}, /*index=5*/s32[]{:T(128...) while((s32[]{:T(128)}, f32[1024]{0:T(1024)S(1)}, ...), condition=%wide.region_5.5_spmd.clone, body=%wide.region_2.4_spmd.clone.sunk | while | flops 25318408 | bytes 2185531 | solution.py:145
  213.9 69.9 %while.69 = (s32[]{:T(128)}, f32[1024]{0:T(1024)S(1)}, f32[1024,3]{0,1:T(4,128)S(1)}, f32[32,9,128]{2,1,0:T(8,128)S(1)}, s32[]{:T(128)}, /*index=5*/f32[32,9,128...) while((s32[]{:T(128)}, f32[1024]{0:T(1024)S(1)}, ...), condition=%wide.region_18.18_spmd.clone, body=%wide.region_6.17_spmd.clone.sunk | while | flops 88628880 | bytes 13360023 | solution.py:177
  288.1 30.1 %while.68 = (s32[]{:T(128)}, f32[1024]{0:T(1024)S(1)}, f32[1024,3]{0,1:T(4,128)S(1)}, s32[]{:T(128)}, f32[32,9,128]{2,1,0:T(8,128)S(1)}, /*index=5*/s32[]{:T(128...) while((s32[]{:T(128)}, f32[1024]{0:T(1024)S(1)}, ...), condition=%wide.region_5.5_spmd.clone, body=%wide.region_2.4_spmd.clone.sunk | while | flops 25318408 | bytes 2185531 | solution.py:145
  318.2 83.8 %while.69 = (s32[]{:T(128)}, f32[1024]{0:T(1024)S(1)}, f32[1024,3]{0,1:T(4,128)S(1)}, f32[32,9,128]{2,1,0:T(8,128)S(1)}, s32[]{:T(128)}, /*index=5*/f32[32,9,128...) while((s32[]{:T(128)}, f32[1024]{0:T(1024)S(1)}, ...), condition=%wide.region_18.18_spmd.clone, body=%wide.region_6.17_spmd.clone.sunk | while | flops 88628880 | bytes 13360023 | solution.py:177
  406.2 25.2 %while.68 = (s32[]{:T(128)}, f32[1024]{0:T(1024)S(1)}, f32[1024,3]{0,1:T(4,128)S(1)}, s32[]{:T(128)}, f32[32,9,128]{2,1,0:T(8,128)S(1)}, /*index=5*/s32[]{:T(128...) while((s32[]{:T(128)}, f32[1024]{0:T(1024)S(1)}, ...), condition=%wide.region_5.5_spmd.clone, body=%wide.region_2.4_spmd.clone.sunk | while | flops 25318408 | bytes 2185531 | solution.py:145
  431.5 69.9 %while.69 = (s32[]{:T(128)}, f32[1024]{0:T(1024)S(1)}, f32[1024,3]{0,1:T(4,128)S(1)}, f32[32,9,128]{2,1,0:T(8,128)S(1)}, s32[]{:T(128)}, /*index=5*/f32[32,9,128...) while((s32[]{:T(128)}, f32[1024]{0:T(1024)S(1)}, ...), condition=%wide.region_18.18_spmd.clone, body=%wide.region_6.17_spmd.clone.sunk | while | flops 88628880 | bytes 13360023 | solution.py:177
  505.6 37.5 %while.68 = (s32[]{:T(128)}, f32[1024]{0:T(1024)S(1)}, f32[1024,3]{0,1:T(4,128)S(1)}, s32[]{:T(128)}, f32[32,9,128]{2,1,0:T(8,128)S(1)}, /*index=5*/s32[]{:T(128...) while((s32[]{:T(128)}, f32[1024]{0:T(1024)S(1)}, ...), condition=%wide.region_5.5_spmd.clone, body=%wide.region_2.4_spmd.clone.sunk | while | flops 25318408 | bytes 2185531 | solution.py:145
  543.1 104.6 %while.69 = (s32[]{:T(128)}, f32[1024]{0:T(1024)S(1)}, f32[1024,3]{0,1:T(4,128)S(1)}, f32[32,9,128]{2,1,0:T(8,128)S(1)}, s32[]{:T(128)}, /*index=5*/f32[32,9,128...) while((s32[]{:T(128)}, f32[1024]{0:T(1024)S(1)}, ...), condition=%wide.region_18.18_spmd.clone, body=%wide.region_6.17_spmd.clone.sunk | while | flops 88628880 | bytes 13360023 | solution.py:177
  648.8 6.0 broadcast_in_dim.29
  654.8 14.5 scatter_fusion
  669.3 1428.7 %reduce-scatter.2.cloned.1.call-done = f32[16,9,128]{2,1,0:T(8,128)} async-done(((f32[2048,9,128]{2,1,0:T(8,128)}), f32[16,9,128]{2,1,0:T(8,128)}) %reduce-scatter.2.cloned.1.call-update) | async-done | bytes 73744 | tf_op jit(solution)/shard_map/reduce_scatter | solution.py:210
  2103.0 1.9 fusion.80
  2108.1 2.0 pad_add_fusion
  (1466 shorter events, 403.9 us)
Async XLA Ops:
  23.9 126.8 %all-to-all-start = ((f32[128,16,9,128]{3,1,2,0:T(8,128)}), f32[128,16,9,128]{3,1,2,0:T(8,128)}, u32[]{:S(2)}, u32[]{:S(2)}) async-start(f32[128,16,9,128]{3,1,2,0:T(8,128)} %stack.38), calls=%async_computation | async-start | bytes 18874368 | tf_op jit(solution)/shard_map/all_to_all | solution.py:186
  35.5 2062.5 %reduce-scatter.2.cloned.1.call-start = ((), (), s32[]{:S(2)}) async-start(), calls=%async_computation.2 | async-start | bytes 16908288 | tf_op jit(solution)/shard_map/reduce_scatter | solution.py:210
  648.5 1453.6 %copy-start.2 = (f32[4,2048]{1,0:T(4,128)S(1)}, f32[4,2048]{1,0:T(4,128)}, u32[]{:S(2)}) copy-start(f32[4,2048]{1,0:T(4,128)} %copy-done.1) | copy-start | bytes 98308
  648.5 1453.6 %copy-start.5 = (f32[1,2048]{1,0:T(1,128)S(1)}, f32[1,2048]{1,0:T(1,128)}, u32[]{:S(2)}) copy-start(f32[1,2048]{1,0:T(1,128)} %copy-done.4) | copy-start | bytes 24580
  648.5 1453.6 %copy-start.15 = (f32[3,2048]{1,0:T(4,128)S(1)}, f32[3,2048]{1,0:T(4,128)}, u32[]{:S(2)}) copy-start(f32[3,2048]{1,0:T(4,128)} %copy-done.14) | copy-start | bytes 73732
  648.5 1453.6 %copy-start.37 = (f32[1,2048]{1,0:T(1,128)S(1)}, f32[1,2048]{1,0:T(1,128)}, u32[]{:S(2)}) copy-start(f32[1,2048]{1,0:T(1,128)} %get-tuple-element.376) | copy-start | bytes 24580
  648.6 1453.6 %copy-start.38 = (f32[1,2048]{1,0:T(1,128)S(1)}, f32[1,2048]{1,0:T(1,128)}, u32[]{:S(2)}) copy-start(f32[1,2048]{1,0:T(1,128)} %get-tuple-element.386) | copy-start | bytes 24580
  648.6 1453.6 %copy-start.48 = (f32[1,2048]{1,0:T(1,128)S(1)}, f32[1,2048]{1,0:T(1,128)}, u32[]{:S(2)}) copy-start(f32[1,2048]{1,0:T(1,128)} %get-tuple-element.370) | copy-start | bytes 24580
  648.6 1454.0 %copy-start = (f32[59,2048]{1,0:T(8,128)S(1)}, f32[59,2048]{1,0:T(8,128)}, u32[]{:S(2)}) copy-start(f32[59,2048]{1,0:T(8,128)} %param.10) | copy-start | bytes 1449988
  648.6 1454.0 %copy-start.44 = (f32[2048]{0:T(1024)S(1)}, f32[2048]{0:T(1024)}, u32[]{:S(2)}) copy-start(f32[2048]{0:T(1024)} %get-tuple-element.492) | copy-start | bytes 24580
  648.6 1454.1 %copy-start.36 = (f32[2048]{0:T(1024)S(1)}, f32[2048]{0:T(1024)}, u32[]{:S(2)}) copy-start(f32[2048]{0:T(1024)} %copy-done.35) | copy-start | bytes 24580
  648.7 1454.1 %copy-start.34 = (f32[2048]{0:T(1024)S(1)}, f32[2048]{0:T(1024)}, u32[]{:S(2)}) copy-start(f32[2048]{0:T(1024)} %copy-done.33) | copy-start | bytes 24580
  648.7 1454.2 %copy-start.47 = (f32[1,2048]{1,0:T(1,128)S(1)}, f32[1,2048]{1,0:T(1,128)}, u32[]{:S(2)}) copy-start(f32[1,2048]{1,0:T(1,128)} %get-tuple-element.371) | copy-start | bytes 24580
  648.7 1454.2 %copy-start.46 = (f32[1,2048]{1,0:T(1,128)S(1)}, f32[1,2048]{1,0:T(1,128)}, u32[]{:S(2)}) copy-start(f32[1,2048]{1,0:T(1,128)} %get-tuple-element.373) | copy-start | bytes 24580
  648.7 1454.2 %copy-start.45 = (f32[1,2048]{1,0:T(1,128)S(1)}, f32[1,2048]{1,0:T(1,128)}, u32[]{:S(2)}) copy-start(f32[1,2048]{1,0:T(1,128)} %get-tuple-element.375) | copy-start | bytes 24580
  648.7 1454.2 %copy-start.43 = (f32[1,2048]{1,0:T(1,128)S(1)}, f32[1,2048]{1,0:T(1,128)}, u32[]{:S(2)}) copy-start(f32[1,2048]{1,0:T(1,128)} %get-tuple-element.379) | copy-start | bytes 24580
  648.7 1454.2 %copy-start.42 = (f32[1,2048]{1,0:T(1,128)S(1)}, f32[1,2048]{1,0:T(1,128)}, u32[]{:S(2)}) copy-start(f32[1,2048]{1,0:T(1,128)} %get-tuple-element.385) | copy-start | bytes 24580
  648.7 1454.3 %copy-start.41 = (f32[1,2048]{1,0:T(1,128)S(1)}, f32[1,2048]{1,0:T(1,128)}, u32[]{:S(2)}) copy-start(f32[1,2048]{1,0:T(1,128)} %get-tuple-element.382) | copy-start | bytes 24580
  648.7 1454.3 %copy-start.16 = (f32[1,2048]{1,0:T(1,128)S(1)}, f32[1,2048]{1,0:T(1,128)}, u32[]{:S(2)}) copy-start(f32[1,2048]{1,0:T(1,128)} %get-tuple-element.380) | copy-start | bytes 24580
  648.7 1454.3 %copy-start.17 = (f32[1,2048]{1,0:T(1,128)S(1)}, f32[1,2048]{1,0:T(1,128)}, u32[]{:S(2)}) copy-start(f32[1,2048]{1,0:T(1,128)} %get-tuple-element.383) | copy-start | bytes 24580
  648.7 1454.3 %copy-start.18 = (f32[1,2048]{1,0:T(1,128)S(1)}, f32[1,2048]{1,0:T(1,128)}, u32[]{:S(2)}) copy-start(f32[1,2048]{1,0:T(1,128)} %get-tuple-element.365) | copy-start | bytes 24580
  648.8 1458.3 %copy-start.28 = (f32[1,2048]{1,0:T(1,128)S(1)}, f32[1,2048]{1,0:T(1,128)}, u32[]{:S(2)}) copy-start(f32[1,2048]{1,0:T(1,128)} %copy-done.27) | copy-start | bytes 24580
  648.8 1458.3 %copy-start.30 = (f32[1,2048]{1,0:T(1,128)S(1)}, f32[1,2048]{1,0:T(1,128)}, u32[]{:S(2)}) copy-start(f32[1,2048]{1,0:T(1,128)} %copy-done.29) | copy-start | bytes 24580
  648.8 1458.3 %copy-start.32 = (f32[1,2048]{1,0:T(1,128)S(1)}, f32[1,2048]{1,0:T(1,128)}, u32[]{:S(2)}) copy-start(f32[1,2048]{1,0:T(1,128)} %copy-done.31) | copy-start | bytes 24580
  (35 other events, 22717.9 us)
Sparse Core Ops, SparseCore 0:
  669.4 1428.5 reduce-scatter.1
